TPU v7x, 32 devices: a whole 2x2x4 slice. The times are simulated.
32 devices in a mesh: ctx: 8 (over z, y), head: 4 (over x, core).
Axes of the slice: x: 2, y: 2, z: 4, core: 2. Of those that a mesh axis runs over, the one named last changes fastest.
Arguments:
- x_in: bfloat16 [4096, 8192], P('ctx', 'head'), may hold values from -6 to 6
- z_in: bfloat16 [4096, 8192], P('ctx', 'head'), may hold values from -6 to 6
- bc_in: bfloat16 [4096, 256], P('ctx', 'head'), may hold values from -6 to 6
- dt: float32 [4096, 128], P('ctx', 'head'), may hold values from 4.8828125e-05 to 0.25146484, as said below
- decay_scale: float32 [128], P('head'), may hold values from 0.5 to 2
- conv_x: bfloat16 [4, 8192], P(None, 'head'), may hold values from -3 to 3
- conv_bc: bfloat16 [4, 256], P(None, 'head'), may hold values from -3 to 3
- norm_gain: bfloat16 [8192], P('head'), may hold values from 0.25 to 1.75
- doc_start: int32 [4096], P('ctx'), may hold values from 0 to 1, as said below
Outputs:
- out: bfloat16 [4096, 8192], P('ctx', 'head')
Inputs may be any that keep to these rules, and one draw needn't show every extreme that they name: doc_start[0] = 0; going round the loop, two consecutive ones are at most 512 apart; the document that holds position 0 is exactly 512 long and begins 3 (4 - 1) or more positions before the end. `dt`: positive step sizes.
All inputs are finite; a program needn't handle non-finite values.
Results may differ from a plain program's by a relative error of at most 0.0034.
Values may be sent and summed in bfloat16 or wider, within the bound.
No kernel may reach another device: no remote copies, remote signals or barrier semaphores. Data moves between devices by JAX's collectives and lax.ppermute only.
A program may use at most 64 MiB of HBM per device.

v0:
```python
import jax
import jax.numpy as jnp
from jax import lax
from jax.sharding import PartitionSpec as P

HDIM = 64
DSTATE = 128
BLOCK = 256
CONV = 4


def shifted(value, axis, steps):
    count = lax.axis_size(axis)
    pairs = [(source, (source + steps) % count) for source in range(count)]
    return lax.ppermute(value, axis, pairs)


def causal_conv(padded, taps, same):
    rows = same.shape[1]
    total = jnp.zeros((rows, taps.shape[1]), jnp.float32)
    for offset in range(taps.shape[0]):
        piece = padded[offset : offset + rows].astype(jnp.float32) * taps[offset].astype(
            jnp.float32
        )
        total = total + jnp.where(same[offset][:, None], piece, 0.0)
    return jax.nn.silu(total)


def block_pass(state, values, bmat, cmat, steps, scale, doc_ids, doc_before):
    high = lax.Precision.HIGHEST
    log_decay = jnp.cumsum(-steps * scale[None, :], axis=0)
    scores = jnp.dot(cmat, bmat.T, precision=high)
    rows = doc_ids.shape[0]
    lower = jnp.arange(rows)[:, None] >= jnp.arange(rows)[None, :]
    keep = lower & (doc_ids[:, None] == doc_ids[None, :])
    decay_t = log_decay.T
    spread = decay_t[:, :, None] - decay_t[:, None, :]
    weights = (
        jnp.where(keep[None, :, :], jnp.exp(jnp.minimum(spread, 0.0)), 0.0) * scores[None, :, :]
    )
    output = jnp.einsum("hts,shp->htp", weights, values, precision=high)
    live = doc_ids == doc_before
    carried = jnp.einsum("tn,hpn->htp", cmat, state, precision=high)
    output = output + jnp.where(live[None, :, None], jnp.exp(decay_t)[:, :, None] * carried, 0.0)
    tail = doc_ids == doc_ids[-1]
    to_end = jnp.where(tail[:, None], jnp.exp(log_decay[-1][None, :] - log_decay), 0.0)
    fresh = jnp.einsum("sh,shp,sn->hpn", to_end, values, bmat, precision=high)
    keep_state = jnp.where(doc_ids[-1] == doc_before, jnp.exp(log_decay[-1]), 0.0)
    return (keep_state[:, None, None] * state + fresh, output)


def gated_norm(output, gate, gain):
    rows, heads, width = output.shape
    mixed = output * jax.nn.silu(gate.astype(jnp.float32)).reshape(rows, heads, width)
    factor = lax.rsqrt(jnp.mean(mixed * mixed, axis=-1, keepdims=True) + 1e-05)
    normed = mixed * factor * gain.astype(jnp.float32).reshape(heads, width)
    return normed.reshape(rows, heads * width).astype(jnp.bfloat16)


def on_device(x_in, z_in, bc_in, dt, decay_scale, conv_x, conv_bc, norm_gain, doc_start):
    high = lax.Precision.HIGHEST
    positions = x_in.shape[0]
    local_heads = dt.shape[1]
    lead = CONV - 1
    doc_ids = jnp.cumsum(doc_start)
    in_last = (doc_ids[-lead:] == doc_ids[-1])[:, None]
    tail_x = jnp.where(in_last, x_in[-lead:], jnp.zeros_like(x_in[-lead:]))
    tail_bc = jnp.where(in_last, bc_in[-lead:], jnp.zeros_like(bc_in[-lead:]))
    rim_x, rim_bc = shifted((tail_x, tail_bc), "ctx", 1)
    x_pad = jnp.concatenate([rim_x, x_in], axis=0)
    bc_pad = jnp.concatenate([rim_bc, bc_in], axis=0)
    ids_pad = jnp.concatenate([jnp.zeros((lead,), jnp.int32), doc_ids], axis=0)
    same = jnp.stack([ids_pad[offset : offset + positions] == doc_ids for offset in range(CONV)])
    x_conv = causal_conv(x_pad, conv_x, same)
    bc_local = causal_conv(bc_pad, conv_bc, same).astype(jnp.bfloat16)
    bc_whole = lax.all_gather(bc_local, "head", axis=1, tiled=True).astype(jnp.float32)
    bmat = bc_whole[:, :DSTATE]
    cmat = bc_whole[:, DSTATE:]
    blocks = positions // BLOCK
    empty = jnp.zeros((local_heads, HDIM, DSTATE), jnp.float32)
    end_state = empty
    pieces = []
    for index in range(blocks):
        low = index * BLOCK
        high_end = low + BLOCK
        before = jnp.full((), -1, jnp.int32) if index == 0 else doc_ids[low - 1]
        block_values = x_conv[low:high_end].reshape(BLOCK, local_heads, HDIM)
        end_state, block_out = block_pass(
            end_state,
            block_values,
            bmat[low:high_end],
            cmat[low:high_end],
            dt[low:high_end],
            decay_scale,
            doc_ids[low:high_end],
            before,
        )
        pieces.append(block_out)
    output = jnp.concatenate(pieces, axis=1)
    device_decay = jnp.cumsum(-dt * decay_scale[None, :], axis=0)
    through = jnp.where(doc_ids[-1] == 0, jnp.exp(device_decay[-1]), 0.0)

    def relay_turn(turn, incoming):
        return shifted(through[:, None, None] * incoming + end_state, "ctx", 1)

    state_in = lax.fori_loop(0, lax.axis_size("ctx") // 8, relay_turn, empty)
    carried = jnp.einsum("tn,hpn->htp", cmat, state_in, precision=high)
    live = (doc_ids == 0)[None, :, None]
    output = output + jnp.where(live, jnp.exp(device_decay.T)[:, :, None] * carried, 0.0)
    return gated_norm(jnp.transpose(output, (1, 0, 2)), z_in, norm_gain)


def solution(mesh):
    in_specs = (
        P("ctx", "head"),
        P("ctx", "head"),
        P("ctx", "head"),
        P("ctx", "head"),
        P("head"),
        P(None, "head"),
        P(None, "head"),
        P("head"),
        P("ctx"),
    )
    out_specs = P("ctx", "head")
    return jax.shard_map(
        on_device, mesh=mesh, in_specs=in_specs, out_specs=out_specs, check_vma=False
    )
```

profile of v0, /device:TPU:0, one launch (start us, length us, event | category | flops | bytes accessed | tf_op | source)
XLA Modules:
  0.0 98.0 jit_solution(13949360632276049648)
XLA Ops:
  0.0 1.0 %reduce-window.29 = s32[4,128]{1,0:T(4,128)S(1)} reduce-window(s32[4,128]{1,0:T(4,128)} %bitcast.145, s32[]{:T(128)} %constant.12.clone.1), window={size=1x128 pad=0_0x127_0}, to_apply=%region_0.0 | reduce-window | flops 65024 | bytes 4100 | tf_op jit(solution)/shard_map/reduce-window
  1.0 0.1 slice.151
  1.1 0.1 slice_reduce_fusion.5
  1.2 0.6 broadcast_compare_fusion
  1.8 0.6 fusion.84
  2.4 0.7 slice_compare_fusion
  3.1 0.8 slice_select_fusion.1
  3.9 3.0 %collective-permute-start = (bf16[3,64]{0,1:T(8,128)(2,1)S(1)}, bf16[3,64]{0,1:T(8,128)(2,1)S(1)}, u32[]{:S(2)}, u32[]{:S(2)}) collective-permute-start(bf16[3,64]{0,1:T(8,128)(2,1)S(1)} %slice_select_fusion.1), channel_id=1, source_target_pairs={{0,4},{4,8},{8,12},{12,16},{16,20},{20,24},{24,28},{28,0},{1,5},{5... | collective-permute-start | bytes 1160 | tf_op jit(solution)/shard_map/ppermute | solution.py:15
  6.9 0.8 slice_select_fusion
  7.7 1.6 %collective-permute-start.1 = (bf16[3,2048]{1,0:T(4,128)(2,1)S(1)}, bf16[3,2048]{1,0:T(4,128)(2,1)S(1)}, u32[]{:S(2)}, u32[]{:S(2)}) collective-permute-start(bf16[3,2048]{1,0:T(4,128)(2,1)S(1)} %slice_select_fusion), channel_id=1, source_target_pairs={{0,4},{4,8},{8,12},{12,16},{16,20},{20,24},{24,28},{28,0},{1,5},{5... | collective-permute-start | bytes 36872 | tf_op jit(solution)/shard_map/ppermute | solution.py:15
  9.3 0.1 fusion.72
  9.4 0.7 slice.189
  10.0 0.6 slice.194
  10.6 0.8 fusion.50
  11.4 0.8 multiply_bitcast_fusion.1
  12.3 0.6 reduce-window.35
  12.9 0.2 slice_reduce_fusion.1
  13.1 0.7 fusion.82
  13.8 0.7 fusion.81
  15.1 0.9 copy_bitcast_fusion
  16.0 0.6 reduce-window.31
  16.6 0.2 slice_reduce_fusion.2
  16.8 0.7 copy_bitcast_fusion.2
  17.5 0.7 fusion.79
  18.1 1.1 %reduce-window.39 = f32[32,4,128]{2,0,1:T(8,128)S(1)} reduce-window(f32[32,4,128]{2,0,1:T(8,128)S(1)} %copy_bitcast_fusion, f32[]{:T(128)} %constant.13.clone.1), window={size=1x1x128 pad=0_0x0_0x127_0}, to_apply=%region_6.7 | reduce-window | flops 2080768 | bytes 131076 | tf_op jit(solution)/shard_map/reduce-window.6
  19.3 0.2 slice_reduce_fusion
  19.5 0.1 bitcast_bitcast_fusion
  19.6 0.1 bitcast_exponential_fusion
  19.7 0.8 bitcast_convert_fusion.3
  21.7 2.5 %broadcast_compare_fusion.1 = (pred[256]{0:T(512)(128)(4,1)S(1)}, pred[256]{0:T(512)(128)(4,1)}, pred[256]{0:T(512)(128)(4,1)S(1)}, pred[256]{0:T(512)(128)(4,1)}) fusion(s32[]{:T(128)} %bitcast.27, s32[4,128]{1,0:T(4,128)S(1)} %get-tuple-element.16, s32[]{:T(128)} %bitcast.19, s32[]{:T(128)} %bitcast.20), kind=kLoop, calls=%fused_computation.127 | loop fusion | flops 1024 | bytes 3084 | tf_op jit(solution)/shard_map/eq | solution.py:45
  24.2 0.2 slice_reduce_fusion.4
  24.4 0.9 slice_convert_fusion.3
  26.0 0.1 exponential_select_fusion.1
  26.1 0.5 fusion.75
  26.6 0.2 slice_reduce_fusion.3
  26.8 0.1 exponential_select_fusion
  26.9 0.5 broadcast_select_fusion
  27.4 4.7 %convert_multiply_fusion = f32[512,2048]{1,0:T(8,128)} fusion(bf16[512,2048]{1,0:T(8,128)(2,1)} %param.10), kind=kLoop, calls=%fused_computation.12 | loop fusion | flops 5242880 | bytes 6291456 | tf_op jit(solution)/shard_map/jit(silu)/mul | solution.py:54
  32.0 0.8 fusion.71
  32.8 5.5 %copy.68 = f32[512,2048]{0,1:T(8,128)} copy(f32[512,2048]{1,0:T(8,128)} %convert_multiply_fusion) | data formatting | bytes 8388608 | tf_op jit(solution)/shard_map/jit(silu)/mul | solution.py:54
  38.3 0.0 copy-done.15
  38.3 0.1 reshape.296
  38.4 0.0 collective-permute-done
  38.4 0.2 multiply_convert_fusion.1
  38.6 5.8 %all_gather.3 = bf16[512,256]{0,1:T(8,128)(2,1)S(1)} all-gather(bf16[512,64]{0,1:T(8,128)(2,1)S(1)} %multiply_convert_fusion.1), channel_id=1, replica_groups=mesh['ctx'=8,'head'=4] {'head'}, dimensions={1}, use_global_device_ids=true | all-gather | bytes 327680 | tf_op jit(solution)/shard_map/all_gather | solution.py:76
  44.4 0.9 fusion.59
  45.3 2.3 %fusion.48 = f32[32,64,256]{2,1,0:T(8,128)} fusion(bf16[512,256]{0,1:T(8,128)(2,1)S(1)} %all_gather.3), kind=kOutput, calls=%fused_computation.49 | convolution fusion | flops 805306368 | bytes 2162688 | tf_op jit(solution)/shard_map/tn,hpn->htp/dot_general | solution.py:43
  47.6 0.9 fusion.64
  48.5 0.0 collective-permute-done.1
  48.5 4.2 %divide_multiply_fusion = f32[512,2048]{1,0:T(8,128)S(1)} fusion(bf16[512,2048]{1,0:T(8,128)(2,1)S(1)} %copy-done.3, bf16[3,2048]{1,0:T(4,128)(2,1)S(1)} %collective-permute-done.1, f32[2048]{0:T(1024)S(1)} %bitcast.143, f32[2048]{0:T(1024)S(1)} %bitcast.144, f32[2048]{0:T(1024)S(1)} %bitcast.142, f32[2048]{0:T(1024)S(1)} %bitcast.141, ...), kind=kLoop, calls=%fused_computation.25 | loop fusion | flops 28311552 | bytes 6338048 | tf_op jit(solution)/shard_map/jit(silu)/mul | solution.py:26
  52.7 2.3 %fusion.83 = (f32[256,2048]{1,0:T(8,128)}, f32[256,2048]{1,0:T(8,128)}) fusion(f32[512,2048]{1,0:T(8,128)S(1)} %divide_multiply_fusion), kind=kLoop, calls=%fused_computation.139 | loop fusion | bytes 8388608 | tf_op jit(solution)/shard_map/slice | solution.py:87
  55.0 1.9 %copy.59 = f32[256,2048]{0,1:T(8,128)S(1)} copy(f32[256,2048]{1,0:T(8,128)} %get-tuple-element.20) | data formatting | bytes 4194304 | tf_op jit(solution)/shard_map/slice | solution.py:87
  56.9 1.7 %fusion.37 = f32[32,64,128]{2,1,0:T(8,128)S(1)} fusion(f32[256,32,64]{0,2,1:T(8,128)S(1)} %bitcast.136, f32[256,32]{0,1:T(8,128)S(1)} %exponential_select_fusion.1, f32[32]{0:T(128)} %fusion.75, bf16[512,256]{0,1:T(8,128)(2,1)S(1)} %all_gather.3), kind=kOutput, calls=%fused_computation.44 | convolution fusion | flops 806092800 | bytes 3244160 | tf_op jit(solution)/shard_map/sh,shp,sn->hpn/dot_general | solution.py:47
  58.7 2.4 %fusion.55 = f32[32,64,256]{2,1,0:T(8,128)} fusion(f32[32,64,128]{2,1,0:T(8,128)S(1)} %fusion.37, bf16[512,256]{0,1:T(8,128)(2,1)S(1)} %all_gather.3), kind=kOutput, calls=%fused_computation.68 | convolution fusion | flops 805306368 | bytes 3211264 | tf_op jit(solution)/shard_map/tn,hpn->htp/dot_general | solution.py:43
  61.0 0.0 copy-done.1
  61.0 1.9 %copy.64 = f32[256,2048]{0,1:T(8,128)S(1)} copy(f32[256,2048]{1,0:T(8,128)} %get-tuple-element.18) | data formatting | bytes 4194304 | tf_op jit(solution)/shard_map/slice | solution.py:87
  63.0 1.1 %fusion.43 = f32[32,64,128]{2,1,0:T(8,128)S(1)} fusion(f32[256,32,64]{0,2,1:T(8,128)S(1)} %bitcast.134, f32[256,32]{0,1:T(8,128)S(1)} %exponential_select_fusion, f32[32,64,128]{2,1,0:T(8,128)S(1)} %fusion.37, f32[32]{0:T(128)S(1)} %copy-done.18, f32[32]{0:T(128)S(1)} %copy-done.17, bf16[512,256]{0,1:T(8,128)(2,1)S(1)} %all_gather.3), kind=kOutput, calls=%fused_computation.46 | convolution fusion | flops 806617088 | bytes 4293632 | tf_op jit(solution)/shard_map/sh,shp,sn->hpn/dot_general | solution.py:47
  64.2 1.8 %collective-permute-start.2 = (f32[32,64,128]{2,1,0:T(8,128)S(1)}, f32[32,64,128]{2,1,0:T(8,128)S(1)}, u32[]{:S(2)}, u32[]{:S(2)}) collective-permute-start(f32[32,64,128]{2,1,0:T(8,128)S(1)} %fusion.43), channel_id=1, source_target_pairs={{0,4},{4,8},{8,12},{12,16},{16,20},{20,24},{24,28},{28,0},{1,5},{5... | collective-permute-start | bytes 3145736 | tf_op jit(solution)/shard_map/while/body/eval_jaxpr/ppermute | solution.py:15
  66.0 10.0 %bitcast_add_fusion = f32[32,256,64]{1,2,0:T(8,128)S(1)} fusion(f32[32,64,256]{2,1,0:T(8,128)S(1)} %copy-done.5, f32[256,32,64]{0,2,1:T(8,128)S(1)} %bitcast.135, f32[256,256]{1,0:T(8,128)S(1)} %copy-done.7, f32[32,256]{1,0:T(8,128)S(1)} %copy-done.11, pred[256,256]{1,0:T(8,128)(4,1)S(1)} %copy-done.10, f32[32,256]{1,0:T(8,128)S(1)} %copy-done.13, ...), kind=kOutput, calls=%fused_computation.38 | convolution fusion | flops 1620574208 | bytes 6684928 | tf_op jit(solution)/shard_map/hts,shp->htp/dot_general | solution.py:41
  76.1 10.2 %bitcast_add_fusion.1 = f32[32,256,64]{1,2,0:T(8,128)S(1)} fusion(f32[32,64,256]{2,1,0:T(8,128)S(1)} %copy-done.4, f32[256,32,64]{0,2,1:T(8,128)S(1)} %bitcast.137, f32[256,256]{1,0:T(8,128)S(1)} %copy-done.6, f32[32,256]{1,0:T(8,128)S(1)} %copy-done.12, pred[256,256]{1,0:T(8,128)(4,1)S(1)} %copy-done.9, f32[32,256]{1,0:T(8,128)S(1)} %copy-done.14, ...), kind=kOutput, calls=%fused_computation.39 | convolution fusion | flops 1620574208 | bytes 6684928 | tf_op jit(solution)/shard_map/hts,shp->htp/dot_general | solution.py:41
  86.3 6.2 %collective-permute-done.2 = f32[32,64,128]{2,1,0:T(8,128)S(1)} collective-permute-done((f32[32,64,128]{2,1,0:T(8,128)S(1)}, f32[32,64,128]{2,1,0:T(8,128)S(1)}, u32[]{:S(2)}, u32[]{:S(2)}) %collective-permute-start.2) | collective-permute-done | bytes 1048608 | tf_op jit(solution)/shard_map/while/body/eval_jaxpr/ppermute | solution.py:15
  92.5 2.5 %multiply_reduce_fusion = (f32[512,32]{0,1:T(8,128)S(1)}, f32[512,32,64]{0,2,1:T(8,128)S(1)}) fusion(f32[512,32,64]{0,2,1:T(8,128)S(1)} %bitcast.132, f32[32,64,128]{2,1,0:T(8,128)S(1)} %collective-permute-done.2, bf16[512,256]{0,1:T(8,128)(2,1)S(1)} %all_gather.3, f32[32,512]{1,0:T(8,128)S(1)} %bitcast_exponential_fusion, ...), kind=kOutput, calls=%fused_computation.21 | convolution fusion | flops 1617936384 | bytes 13894144 | tf_op jit(solution)/shard_map/tn,hpn->htp/dot_general | solution.py:107
  95.1 0.5 multiply_convert_fusion
  95.6 2.4 %copy.69 = bf16[512,2048]{1,0:T(8,128)(2,1)} copy(bf16[512,2048]{0,1:T(8,128)(2,1)S(1)} %bitcast.133) | data formatting | bytes 4194304 | tf_op jit(solution)/shard_map/convert_element_type | solution.py:57
  (50 shorter events, 0.3 us)
Async XLA Ops:
  3.9 34.5 %collective-permute-start = (bf16[3,64]{0,1:T(8,128)(2,1)S(1)}, bf16[3,64]{0,1:T(8,128)(2,1)S(1)}, u32[]{:S(2)}, u32[]{:S(2)}) collective-permute-start(bf16[3,64]{0,1:T(8,128)(2,1)S(1)} %slice_select_fusion.1), channel_id=1, source_target_pairs={{0,4},{4,8},{8,12},{12,16},{16,20},{20,24},{24,28},{28,0},{1,5},{5... | collective-permute-start | bytes 1160 | tf_op jit(solution)/shard_map/ppermute | solution.py:15
  7.7 40.8 %collective-permute-start.1 = (bf16[3,2048]{1,0:T(4,128)(2,1)S(1)}, bf16[3,2048]{1,0:T(4,128)(2,1)S(1)}, u32[]{:S(2)}, u32[]{:S(2)}) collective-permute-start(bf16[3,2048]{1,0:T(4,128)(2,1)S(1)} %slice_select_fusion), channel_id=1, source_target_pairs={{0,4},{4,8},{8,12},{12,16},{16,20},{20,24},{24,28},{28,0},{1,5},{5... | collective-permute-start | bytes 36872 | tf_op jit(solution)/shard_map/ppermute | solution.py:15
  32.8 5.5 %copy-start.15 = (bf16[2048]{0:T(1024)(128)(2,1)S(1)}, bf16[2048]{0:T(1024)(128)(2,1)}, u32[]{:S(2)}) copy-start(bf16[2048]{0:T(1024)(128)(2,1)} %param.16) | copy-start | bytes 12292
  32.8 5.6 %copy-start.8 = (bf16[512,64]{0,1:T(8,128)(2,1)S(1)}, bf16[512,64]{0,1:T(8,128)(2,1)}, u32[]{:S(2)}) copy-start(bf16[512,64]{0,1:T(8,128)(2,1)} %param.11) | copy-start | bytes 196612
  32.8 15.7 %copy-start.3 = (bf16[512,2048]{1,0:T(8,128)(2,1)S(1)}, bf16[512,2048]{1,0:T(8,128)(2,1)}, u32[]{:S(2)}) copy-start(bf16[512,2048]{1,0:T(8,128)(2,1)} %param.9) | copy-start | bytes 6291460
  56.9 4.1 %copy-start.1 = (f32[256,2048]{0,1:T(8,128)}, f32[256,2048]{0,1:T(8,128)S(1)}, u32[]{:S(2)}) copy-start(f32[256,2048]{0,1:T(8,128)S(1)} %copy.59) | copy-start | bytes 6291460
  58.6 4.4 %copy-start.17 = (f32[32]{0:T(128)S(1)}, f32[32]{0:T(128)}, u32[]{:S(2)}) copy-start(f32[32]{0:T(128)} %fusion.71) | copy-start | bytes 388
  58.7 4.4 %copy-start.18 = (f32[32]{0:T(128)S(1)}, f32[32]{0:T(128)}, u32[]{:S(2)}) copy-start(f32[32]{0:T(128)} %broadcast_select_fusion) | copy-start | bytes 388
  63.0 3.0 %copy-start.5 = (f32[32,64,256]{2,1,0:T(8,128)S(1)}, f32[32,64,256]{2,1,0:T(8,128)}, u32[]{:S(2)}) copy-start(f32[32,64,256]{2,1,0:T(8,128)} %fusion.55) | copy-start | bytes 6291460
  63.0 3.0 %copy-start.7 = (f32[256,256]{1,0:T(8,128)S(1)}, f32[256,256]{1,0:T(8,128)}, u32[]{:S(2)}) copy-start(f32[256,256]{1,0:T(8,128)} %fusion.59) | copy-start | bytes 786436
  63.0 2.9 %copy-start.10 = (pred[256,256]{1,0:T(8,128)(4,1)S(1)}, pred[256,256]{1,0:T(8,128)(4,1)}, u32[]{:S(2)}) copy-start(pred[256,256]{1,0:T(8,128)(4,1)} %get-tuple-element.50) | copy-start | bytes 196612
  63.0 2.9 %copy-start.11 = (f32[32,256]{1,0:T(8,128)S(1)}, f32[32,256]{1,0:T(8,128)}, u32[]{:S(2)}) copy-start(f32[32,256]{1,0:T(8,128)} %get-tuple-element.24) | copy-start | bytes 98308
  63.0 2.9 %copy-start.13 = (f32[32,256]{1,0:T(8,128)S(1)}, f32[32,256]{1,0:T(8,128)}, u32[]{:S(2)}) copy-start(f32[32,256]{1,0:T(8,128)} %fusion.81) | copy-start | bytes 98308
  63.0 2.9 %copy-start.20 = (pred[256]{0:T(512)(128)(4,1)S(1)}, pred[256]{0:T(512)(128)(4,1)}, u32[]{:S(2)}) copy-start(pred[256]{0:T(512)(128)(4,1)} %get-tuple-element.32) | copy-start | bytes 772
  64.2 28.3 %collective-permute-start.2 = (f32[32,64,128]{2,1,0:T(8,128)S(1)}, f32[32,64,128]{2,1,0:T(8,128)S(1)}, u32[]{:S(2)}, u32[]{:S(2)}) collective-permute-start(f32[32,64,128]{2,1,0:T(8,128)S(1)} %fusion.43), channel_id=1, source_target_pairs={{0,4},{4,8},{8,12},{12,16},{16,20},{20,24},{24,28},{28,0},{1,5},{5... | collective-permute-start | bytes 3145736 | tf_op jit(solution)/shard_map/while/body/eval_jaxpr/ppermute | solution.py:15
  66.0 10.0 %copy-start.2 = (f32[256,2048]{0,1:T(8,128)S(1)}, f32[256,2048]{0,1:T(8,128)}, u32[]{:S(2)}) copy-start(f32[256,2048]{0,1:T(8,128)} %copy-done.1) | copy-start | bytes 6291460
  66.0 10.0 %copy-start.4 = (f32[32,64,256]{2,1,0:T(8,128)S(1)}, f32[32,64,256]{2,1,0:T(8,128)}, u32[]{:S(2)}) copy-start(f32[32,64,256]{2,1,0:T(8,128)} %fusion.48) | copy-start | bytes 6291460
  66.0 10.0 %copy-start.6 = (f32[256,256]{1,0:T(8,128)S(1)}, f32[256,256]{1,0:T(8,128)}, u32[]{:S(2)}) copy-start(f32[256,256]{1,0:T(8,128)} %fusion.64) | copy-start | bytes 786436
  66.0 10.0 %copy-start.9 = (pred[256,256]{1,0:T(8,128)(4,1)S(1)}, pred[256,256]{1,0:T(8,128)(4,1)}, u32[]{:S(2)}) copy-start(pred[256,256]{1,0:T(8,128)(4,1)} %get-tuple-element.51) | copy-start | bytes 196612
  66.0 10.0 %copy-start.12 = (f32[32,256]{1,0:T(8,128)S(1)}, f32[32,256]{1,0:T(8,128)}, u32[]{:S(2)}) copy-start(f32[32,256]{1,0:T(8,128)} %get-tuple-element.25) | copy-start | bytes 98308
  66.0 10.0 %copy-start.14 = (f32[32,256]{1,0:T(8,128)S(1)}, f32[32,256]{1,0:T(8,128)}, u32[]{:S(2)}) copy-start(f32[32,256]{1,0:T(8,128)} %fusion.79) | copy-start | bytes 98308
  66.0 10.0 %copy-start.19 = (pred[256]{0:T(512)(128)(4,1)S(1)}, pred[256]{0:T(512)(128)(4,1)}, u32[]{:S(2)}) copy-start(pred[256]{0:T(512)(128)(4,1)} %get-tuple-element.34) | copy-start | bytes 772
  76.1 16.5 %copy-start = (f32[512,2048]{0,1:T(8,128)S(1)}, f32[512,2048]{0,1:T(8,128)}, u32[]{:S(2)}) copy-start(f32[512,2048]{0,1:T(8,128)} %copy.68) | copy-start | bytes 12582916
  76.1 16.5 %copy-start.16 = (pred[512]{0:T(512)(128)(4,1)S(1)}, pred[512]{0:T(512)(128)(4,1)}, u32[]{:S(2)}) copy-start(pred[512]{0:T(512)(128)(4,1)} %get-tuple-element.11) | copy-start | bytes 1540
where the time goes:
time: 98.6 us; the launch traced here: 98 us
  matrix products  32 us (32%)
  other arithmetic  27.6 us (28%)
  local copies, waits for them, and re-layouts  17.1 us (17%)
  starting transfers between devices  6.29 us (6%)
  waiting for transfers between devices  6.22 us (6%)
  blocking collectives  5.79 us (6%)
  between operations  2.89 us (3%)
    dot_general x2, matrix products, block_pass(): output = jnp.einsum('hts,shp->htp', weights, values, precision=high)  20.2 us
    ppermute x3, starting transfers between devices, shifted(): return lax.ppermute(value, axis, pairs)  6.29 us
    ppermute x3, waiting for transfers between devices, shifted(): return lax.ppermute(value, axis, pairs)  6.22 us
    slice x3, local copies, waits for them, and re-layouts, on_device(): block_values = x_conv[low:high_end].reshape(BLOCK, local_heads, HDIM)  6.14 us
    another operation x12, other arithmetic  5.84 us
    all_gather x1, blocking collectives, on_device(): lax.all_gather(bc_local, 'head', axis=1, tiled=True).astype(jnp.float32)  5.79 us
    mul x1, local copies, waits for them, and re-layouts, gated_norm(): jax.nn.silu(gate.astype(jnp.float32)).reshape(rows, heads, width)  5.5 us
    dot_general x2, matrix products, block_pass(): carried = jnp.einsum('tn,hpn->htp', cmat, state, precision=high)  4.66 us
  transfers between devices with their start and end apart: 3, of which 1 were waited for; matrix products, arithmetic and copies ran while one was open for 53% of the time, Pallas kernels for 0%

commit v1 on v0

--- a/solution.py
+++ b/solution.py
@@ -7,6 +7,18 @@
 DSTATE = 128
 BLOCK = 256
 CONV = 4
+
+
+def gather_by_bits(array, axis, dim):
+    ways, here = (lax.axis_size(axis), lax.axis_index(axis))
+    grown, reach = (array, 1)
+    while reach < ways:
+        theirs = lax.ppermute(grown, axis, [(d, d ^ reach) for d in range(ways)])
+        mine_first = jnp.concatenate([grown, theirs], axis=dim)
+        theirs_first = jnp.concatenate([theirs, grown], axis=dim)
+        grown = jnp.where(here & reach == 0, mine_first, theirs_first)
+        reach = 2 * reach
+    return grown
 
 
 def shifted(value, axis, steps):
@@ -73,7 +85,7 @@
     same = jnp.stack([ids_pad[offset : offset + positions] == doc_ids for offset in range(CONV)])
     x_conv = causal_conv(x_pad, conv_x, same)
     bc_local = causal_conv(bc_pad, conv_bc, same).astype(jnp.bfloat16)
-    bc_whole = lax.all_gather(bc_local, "head", axis=1, tiled=True).astype(jnp.float32)
+    bc_whole = gather_by_bits(bc_local, "head", 1).astype(jnp.float32)
     bmat = bc_whole[:, :DSTATE]
     cmat = bc_whole[:, DSTATE:]
     blocks = positions // BLOCK

time: 98.6 us -> 84.3 us (0.85)
  other arithmetic: 27.6 us -> 21.6 us
  blocking collectives: 5.79 us -> 0 us
  matrix products: 32 us -> 28.9 us
  starting transfers between devices: 6.29 us -> 7.93 us
  waiting for transfers between devices: 6.22 us -> 5.04 us
    all_gather x1 -> x0, blocking collectives: 5.79 us -> none  [on_device(): lax.all_gather(bc_local, 'head', axis=1, tiled=True).astype(jnp.float32)]
    dot_general x2, matrix products: 4.66 us -> 1.98 us  [block_pass(): carried = jnp.einsum('tn,hpn->htp', cmat, state, precision=high)]
    ppermute x0 -> x2, starting transfers between devices: none -> 1.63 us  [gather_by_bits(): theirs = lax.ppermute(grown, axis, [(d, d ^ reach) for d in range(ways)])]
    dot_general x2, matrix products: 1.85 us -> 0.36 us  [block_pass(): scores = jnp.dot(cmat, bmat.T, precision=high)]
    another operation x12, other arithmetic: 5.84 us -> 4.61 us
    ppermute x3, waiting for transfers between devices: 6.22 us -> 5.04 us  [shifted(): return lax.ppermute(value, axis, pairs)]
    exp x2, other arithmetic: 1.37 us -> 0.19 us  [block_pass(): jnp.exp(decay_t)[:, :, None] * carried]
    dot_general x2, matrix products: 2.81 us -> 3.85 us  [block_pass(): fresh = jnp.einsum('sh,shp,sn->hpn', to_end, values, bmat, precision=high)]
  transfers between devices with their start and end apart: 3 -> 5, of which waited for: 1 -> 1; matrix products, arithmetic and copies ran while one was open for 53% -> 64% of each run, Pallas kernels for 0% -> 0%
where the time goes in v1:
time: 84.3 us; the launch traced here: 83.6 us
  matrix products  28.9 us (34%)
  other arithmetic  21.6 us (26%)
  local copies, waits for them, and re-layouts  17.3 us (21%)
  starting transfers between devices  7.93 us (9%)
  waiting for transfers between devices  5.04 us (6%)
  between operations  2.85 us (3%)
    dot_general x2, matrix products, block_pass(): output = jnp.einsum('hts,shp->htp', weights, values, precision=high)  20.2 us
    ppermute x3, starting transfers between devices, shifted(): return lax.ppermute(value, axis, pairs)  6.3 us
    mul x1, local copies, waits for them, and re-layouts, gated_norm(): jax.nn.silu(gate.astype(jnp.float32)).reshape(rows, heads, width)  5.51 us
    slice x3, local copies, waits for them, and re-layouts, on_device(): block_values = x_conv[low:high_end].reshape(BLOCK, local_heads, HDIM)  5.47 us
    ppermute x3, waiting for transfers between devices, shifted(): return lax.ppermute(value, axis, pairs)  5.04 us
    mul x1, other arithmetic, gated_norm(): jax.nn.silu(gate.astype(jnp.float32)).reshape(rows, heads, width)  4.66 us
    another operation x12, other arithmetic  4.61 us
    mul x1, other arithmetic, causal_conv(): return jax.nn.silu(total)  4.2 us
  transfers between devices with their start and end apart: 5, of which 1 were waited for; matrix products, arithmetic and copies ran while one was open for 64% of the time, Pallas kernels for 0%

profile of v1, /device:TPU:0, one launch (start us, length us, event | category | flops | bytes accessed | tf_op | source)
XLA Modules:
  0.0 83.6 jit_solution(948416082036547305)
XLA Ops:
  0.0 1.0 %reduce-window.29 = s32[4,128]{1,0:T(4,128)S(1)} reduce-window(s32[4,128]{1,0:T(4,128)} %bitcast.140, s32[]{:T(128)} %constant.13.clone.1), window={size=1x128 pad=0_0x127_0}, to_apply=%region_0.0 | reduce-window | flops 65024 | bytes 4100 | tf_op jit(solution)/shard_map/reduce-window
  1.0 0.1 slice.151
  1.1 0.1 slice_reduce_fusion.5
  1.2 0.1 broadcast_compare_fusion
  1.3 0.6 fusion.84
  1.9 0.6 slice_compare_fusion
  2.5 1.0 %copy.44 = bf16[512,64]{1,0:T(8,128)(2,1)S(1)} copy(bf16[512,64]{0,1:T(8,128)(2,1)} %param.11) | data formatting | bytes 131072 | tf_op args[2]
  3.5 0.1 slice_select_fusion.1
  3.5 3.0 %collective-permute-start = (bf16[3,64]{1,0:T(4,128)(2,1)S(1)}, bf16[3,64]{1,0:T(4,128)(2,1)S(1)}, u32[]{:S(2)}, u32[]{:S(2)}) collective-permute-start(bf16[3,64]{1,0:T(4,128)(2,1)S(1)} %slice_select_fusion.1), channel_id=1, source_target_pairs={{0,4},{4,8},{8,12},{12,16},{16,20},{20,24},{24,28},{28,0},{1,5},{5... | collective-permute-start | bytes 1160 | tf_op jit(solution)/shard_map/ppermute | solution.py:27
  6.5 0.8 slice_select_fusion
  7.4 1.6 %collective-permute-start.3 = (bf16[3,2048]{1,0:T(4,128)(2,1)S(1)}, bf16[3,2048]{1,0:T(4,128)(2,1)S(1)}, u32[]{:S(2)}, u32[]{:S(2)}) collective-permute-start(bf16[3,2048]{1,0:T(4,128)(2,1)S(1)} %slice_select_fusion), channel_id=1, source_target_pairs={{0,4},{4,8},{8,12},{12,16},{16,20},{20,24},{24,28},{28,0},{1,5},{5... | collective-permute-start | bytes 36872 | tf_op jit(solution)/shard_map/ppermute | solution.py:27
  8.9 0.1 fusion.72
  9.0 0.7 slice.189
  9.7 0.6 slice.194
  10.3 0.1 fusion.50
  10.4 0.9 %multiply_bitcast_fusion.1 = (f32[4,2,8,128]{3,2,1,0:T(8,128)S(1)}, f32[4,2,8,128]{3,2,1,0:T(8,128)S(1)}) fusion(f32[512,32]{0,1:T(8,128)} %param.12, f32[32]{0:T(128)} %param.13), kind=kLoop, calls=%fused_computation.94 | loop fusion | flops 32768 | bytes 131200
  11.3 0.6 reduce-window.35
  11.9 0.2 slice_reduce_fusion.1
  12.1 0.1 fusion.82
  12.2 0.1 fusion.81
  12.8 0.9 %copy_bitcast_fusion = f32[32,4,128]{2,0,1:T(8,128)S(1)} fusion(f32[512,32]{0,1:T(8,128)} %param.12, f32[32]{0:T(128)} %param.13), kind=kLoop, calls=%fused_computation.65 | loop fusion | flops 32768 | bytes 131200 | tf_op jit(solution)/shard_map/reshape.13
  13.8 0.6 reduce-window.31
  14.3 0.2 slice_reduce_fusion.2
  14.5 0.1 copy_bitcast_fusion.2
  14.6 0.1 fusion.79
  14.7 1.2 %reduce-window.39 = f32[32,4,128]{2,0,1:T(8,128)S(1)} reduce-window(f32[32,4,128]{2,0,1:T(8,128)S(1)} %copy_bitcast_fusion, f32[]{:T(128)} %constant.14.clone.1), window={size=1x1x128 pad=0_0x0_0x127_0}, to_apply=%region_6.7 | reduce-window | flops 2080768 | bytes 131076 | tf_op jit(solution)/shard_map/reduce-window.6
  15.9 0.2 slice_reduce_fusion
  16.1 0.1 bitcast_bitcast_fusion
  16.2 0.1 bitcast_exponential_fusion
  16.3 0.8 bitcast_convert_fusion.3
  18.4 2.0 %broadcast_compare_fusion.1 = (pred[256]{0:T(512)(128)(4,1)S(1)}, pred[256]{0:T(512)(128)(4,1)S(1)}, pred[256]{0:T(512)(128)(4,1)S(1)}, pred[256]{0:T(512)(128)(4,1)S(1)}) fusion(s32[]{:T(128)} %bitcast.27, s32[4,128]{1,0:T(4,128)S(1)} %get-tuple-element.16, s32[]{:T(128)} %bitcast.19, s32[]{:T(128)} %bitcast.20), kind=kLoop, calls=%fused_computation.127 | loop fusion | flops 1024 | bytes 3084 | tf_op jit(solution)/shard_map/eq | solution.py:57
  20.4 0.2 slice_reduce_fusion.4
  20.6 0.9 %slice_convert_fusion.3 = (f32[1,2048]{1,0:T(1,128)S(1)}, f32[1,2048]{1,0:T(1,128)S(1)}, f32[1,2048]{1,0:T(1,128)S(1)}, f32[1,2048]{1,0:T(1,128)S(1)}) fusion(bf16[4,2048]{1,0:T(4,128)(2,1)} %param.14), kind=kLoop, calls=%fused_computation.107 | loop fusion | flops 8192 | bytes 49152 | tf_op jit(solution)/shard_map/mul | solution.py:34
  22.2 0.1 exponential_select_fusion.1
  22.3 0.2 slice_reduce_fusion.3
  22.4 0.1 exponential_select_fusion
  22.6 4.7 %convert_multiply_fusion = f32[512,2048]{1,0:T(8,128)} fusion(bf16[512,2048]{1,0:T(8,128)(2,1)} %param.10), kind=kLoop, calls=%fused_computation.12 | loop fusion | flops 5242880 | bytes 6291456 | tf_op jit(solution)/shard_map/jit(silu)/mul | solution.py:66
  27.2 0.2 fusion.71
  27.4 0.0 copy-start.3
  27.4 0.0 copy-start.2
  27.4 5.5 %copy.53 = f32[512,2048]{0,1:T(8,128)} copy(f32[512,2048]{1,0:T(8,128)} %convert_multiply_fusion) | data formatting | bytes 8388608 | tf_op jit(solution)/shard_map/jit(silu)/mul | solution.py:66
  33.0 0.1 reshape.296
  33.0 0.3 multiply_convert_fusion.1
  33.3 0.1 collective-permute-start.1
  33.4 4.2 %divide_multiply_fusion = f32[512,2048]{1,0:T(8,128)S(1)} fusion(bf16[512,2048]{1,0:T(8,128)(2,1)S(1)} %copy-done.2, bf16[3,2048]{1,0:T(4,128)(2,1)S(1)} %collective-permute-done.3, f32[2048]{0:T(1024)S(1)} %bitcast.138, f32[2048]{0:T(1024)S(1)} %bitcast.139, f32[2048]{0:T(1024)S(1)} %bitcast.137, f32[2048]{0:T(1024)S(1)} %bitcast.136, ...), kind=kLoop, calls=%fused_computation.25 | loop fusion | flops 28311552 | bytes 6338048 | tf_op jit(solution)/shard_map/jit(silu)/mul | solution.py:38
  37.6 0.1 maximum_select_fusion.1
  37.8 1.6 %collective-permute-start.2 = (bf16[512,128]{1,0:T(8,128)(2,1)S(1)}, bf16[512,128]{1,0:T(8,128)(2,1)S(1)}, u32[]{:S(2)}, u32[]{:S(2)}) collective-permute-start(bf16[512,128]{1,0:T(8,128)(2,1)S(1)} %maximum_select_fusion.1), channel_id=1, source_target_pairs={{0,2},{1,3},{2,0},{3,1},{4,6},{5,7},{6,4},{7,5},{8,10},{9,11},{10,... | collective-permute-start | bytes 393224 | tf_op jit(solution)/shard_map/ppermute | solution.py:16
  39.4 1.7 %fusion.83 = (f32[256,2048]{1,0:T(8,128)}, f32[256,2048]{1,0:T(8,128)S(1)}) fusion(f32[512,2048]{1,0:T(8,128)S(1)} %divide_multiply_fusion), kind=kLoop, calls=%fused_computation.139 | loop fusion | bytes 8388608 | tf_op jit(solution)/shard_map/slice | solution.py:99
  41.1 1.9 %copy.47 = f32[256,2048]{0,1:T(8,128)} copy(f32[256,2048]{1,0:T(8,128)S(1)} %get-tuple-element.20) | data formatting | bytes 4194304 | tf_op jit(solution)/shard_map/slice | solution.py:99
  42.9 1.9 %copy.50 = f32[256,2048]{0,1:T(8,128)S(1)} copy(f32[256,2048]{1,0:T(8,128)} %get-tuple-element.18) | data formatting | bytes 4194304 | tf_op jit(solution)/shard_map/slice | solution.py:99
  44.9 0.1 maximum_select_fusion
  44.9 0.2 fusion.60
  45.1 2.7 %fusion.37 = f32[32,64,128]{2,1,0:T(8,128)S(1)} fusion(f32[256,32,64]{0,2,1:T(8,128)} %bitcast.131, f32[256,32]{0,1:T(8,128)S(1)} %exponential_select_fusion.1, f32[32]{0:T(128)S(1)} %fusion.75, bf16[512,256]{1,0:T(8,128)(2,1)S(1)} %maximum_select_fusion), kind=kOutput, calls=%fused_computation.44 | convolution fusion | flops 806092800 | bytes 3244544 | tf_op jit(solution)/shard_map/sh,shp,sn->hpn/dot_general | solution.py:59
  47.8 1.0 %fusion.55 = f32[32,64,256]{2,1,0:T(8,128)S(1)} fusion(f32[32,64,128]{2,1,0:T(8,128)S(1)} %fusion.37, bf16[512,256]{1,0:T(8,128)(2,1)S(1)} %maximum_select_fusion), kind=kOutput, calls=%fused_computation.68 | convolution fusion | flops 805306368 | bytes 3211264 | tf_op jit(solution)/shard_map/tn,hpn->htp/dot_general | solution.py:55
  48.9 1.1 %fusion.43 = f32[32,64,128]{2,1,0:T(8,128)S(1)} fusion(f32[256,32,64]{0,2,1:T(8,128)S(1)} %bitcast.129, f32[256,32]{0,1:T(8,128)S(1)} %exponential_select_fusion, f32[32,64,128]{2,1,0:T(8,128)S(1)} %fusion.37, f32[32]{0:T(128)S(1)} %broadcast_select_fusion, f32[32]{0:T(128)S(1)} %fusion.71, bf16[512,256]{1,0:T(8,128)(2,1)S(1)} %maximum_select_fusion), kind=kOutput, calls=%fused_computation.46 | convolution fusion | flops 806617088 | bytes 4293632 | tf_op jit(solution)/shard_map/sh,shp,sn->hpn/dot_general | solution.py:59
  50.0 1.8 %collective-permute-start.4 = (f32[32,64,128]{2,1,0:T(8,128)S(1)}, f32[32,64,128]{2,1,0:T(8,128)S(1)}, u32[]{:S(2)}, u32[]{:S(2)}) collective-permute-start(f32[32,64,128]{2,1,0:T(8,128)S(1)} %fusion.43), channel_id=1, source_target_pairs={{0,4},{4,8},{8,12},{12,16},{16,20},{20,24},{24,28},{28,0},{1,5},{5... | collective-permute-start | bytes 3145736 | tf_op jit(solution)/shard_map/while/body/eval_jaxpr/ppermute | solution.py:27
  51.8 10.0 %bitcast_add_fusion = f32[32,256,64]{1,2,0:T(8,128)S(1)} fusion(f32[32,64,256]{2,1,0:T(8,128)S(1)} %fusion.55, f32[256,32,64]{0,2,1:T(8,128)S(1)} %bitcast.130, f32[256,256]{1,0:T(8,128)S(1)} %fusion.60, f32[32,256]{1,0:T(8,128)S(1)} %get-tuple-element.24, pred[256,256]{1,0:T(8,128)(4,1)S(1)} %get-tuple-element.50, f32[32,256]{1,0:T(8,128)S(1)} %fusion.81, ...), kind=kOutput, calls=%fused_computation.38 | convolution fusion | flops 1620574208 | bytes 6684928 | tf_op jit(solution)/shard_map/hts,shp->htp/dot_general | solution.py:53
  61.7 0.2 fusion.65
  61.9 1.0 %fusion.48 = f32[32,64,256]{2,1,0:T(8,128)S(1)} fusion(bf16[512,256]{1,0:T(8,128)(2,1)S(1)} %maximum_select_fusion), kind=kOutput, calls=%fused_computation.49 | convolution fusion | flops 805306368 | bytes 2162688 | tf_op jit(solution)/shard_map/tn,hpn->htp/dot_general | solution.py:55
  62.9 10.2 %bitcast_add_fusion.1 = f32[32,256,64]{1,2,0:T(8,128)S(1)} fusion(f32[32,64,256]{2,1,0:T(8,128)S(1)} %fusion.48, f32[256,32,64]{0,2,1:T(8,128)S(1)} %bitcast.132, f32[256,256]{1,0:T(8,128)S(1)} %fusion.65, f32[32,256]{1,0:T(8,128)S(1)} %get-tuple-element.25, pred[256,256]{1,0:T(8,128)(4,1)S(1)} %get-tuple-element.51, f32[32,256]{1,0:T(8,128)S(1)} %fusion.79, ...), kind=kOutput, calls=%fused_computation.39 | convolution fusion | flops 1620574208 | bytes 6684928 | tf_op jit(solution)/shard_map/hts,shp->htp/dot_general | solution.py:53
  73.1 5.0 %collective-permute-done.4 = f32[32,64,128]{2,1,0:T(8,128)S(1)} collective-permute-done((f32[32,64,128]{2,1,0:T(8,128)S(1)}, f32[32,64,128]{2,1,0:T(8,128)S(1)}, u32[]{:S(2)}, u32[]{:S(2)}) %collective-permute-start.4) | collective-permute-done | bytes 1048608 | tf_op jit(solution)/shard_map/while/body/eval_jaxpr/ppermute | solution.py:27
  78.2 2.5 %multiply_reduce_fusion = (f32[512,32]{0,1:T(8,128)S(1)}, f32[512,32,64]{0,2,1:T(8,128)S(1)}) fusion(f32[512,32,64]{0,2,1:T(8,128)S(1)} %bitcast.127, f32[32,64,128]{2,1,0:T(8,128)S(1)} %collective-permute-done.4, bf16[512,256]{1,0:T(8,128)(2,1)S(1)} %maximum_select_fusion, f32[32,512]{1,0:T(8,128)S(1)} %bitcast_exponential_fusion, ...), kind=kOutput, calls=%fused_computation.21 | convolution fusion | flops 1617936384 | bytes 13894144 | tf_op jit(solution)/shard_map/tn,hpn->htp/dot_general | solution.py:119
  80.7 0.5 multiply_convert_fusion
  81.3 2.4 %copy.54 = bf16[512,2048]{1,0:T(8,128)(2,1)} copy(bf16[512,2048]{0,1:T(8,128)(2,1)S(1)} %bitcast.128) | data formatting | bytes 4194304 | tf_op jit(solution)/shard_map/convert_element_type | solution.py:69
  (22 shorter events, 0.2 us)
Async XLA Ops:
  3.5 29.5 %collective-permute-start = (bf16[3,64]{1,0:T(4,128)(2,1)S(1)}, bf16[3,64]{1,0:T(4,128)(2,1)S(1)}, u32[]{:S(2)}, u32[]{:S(2)}) collective-permute-start(bf16[3,64]{1,0:T(4,128)(2,1)S(1)} %slice_select_fusion.1), channel_id=1, source_target_pairs={{0,4},{4,8},{8,12},{12,16},{16,20},{20,24},{24,28},{28,0},{1,5},{5... | collective-permute-start | bytes 1160 | tf_op jit(solution)/shard_map/ppermute | solution.py:27
  7.4 26.1 %collective-permute-start.3 = (bf16[3,2048]{1,0:T(4,128)(2,1)S(1)}, bf16[3,2048]{1,0:T(4,128)(2,1)S(1)}, u32[]{:S(2)}, u32[]{:S(2)}) collective-permute-start(bf16[3,2048]{1,0:T(4,128)(2,1)S(1)} %slice_select_fusion), channel_id=1, source_target_pairs={{0,4},{4,8},{8,12},{12,16},{16,20},{20,24},{24,28},{28,0},{1,5},{5... | collective-permute-start | bytes 36872 | tf_op jit(solution)/shard_map/ppermute | solution.py:27
  27.4 5.5 %copy-start.3 = (bf16[2048]{0:T(1024)(128)(2,1)S(1)}, bf16[2048]{0:T(1024)(128)(2,1)}, u32[]{:S(2)}) copy-start(bf16[2048]{0:T(1024)(128)(2,1)} %param.16) | copy-start | bytes 12292
  27.4 6.0 %copy-start.2 = (bf16[512,2048]{1,0:T(8,128)(2,1)S(1)}, bf16[512,2048]{1,0:T(8,128)(2,1)}, u32[]{:S(2)}) copy-start(bf16[512,2048]{1,0:T(8,128)(2,1)} %param.9) | copy-start | bytes 6291460
  33.3 4.3 %collective-permute-start.1 = (bf16[512,64]{1,0:T(8,128)(2,1)S(1)}, bf16[512,64]{1,0:T(8,128)(2,1)S(1)}, u32[]{:S(2)}, u32[]{:S(2)}) collective-permute-start(bf16[512,64]{1,0:T(8,128)(2,1)S(1)} %multiply_convert_fusion.1), channel_id=1, source_target_pairs={{0,1},{1,0},{2,3},{3,2},{4,5},{5,4},{6,7},{7,6},{8,9},{9,8},{10,11... | collective-permute-start | bytes 196616 | tf_op jit(solution)/shard_map/ppermute | solution.py:16
  37.8 7.0 %collective-permute-start.2 = (bf16[512,128]{1,0:T(8,128)(2,1)S(1)}, bf16[512,128]{1,0:T(8,128)(2,1)S(1)}, u32[]{:S(2)}, u32[]{:S(2)}) collective-permute-start(bf16[512,128]{1,0:T(8,128)(2,1)S(1)} %maximum_select_fusion.1), channel_id=1, source_target_pairs={{0,2},{1,3},{2,0},{3,1},{4,6},{5,7},{6,4},{7,5},{8,10},{9,11},{10,... | collective-permute-start | bytes 393224 | tf_op jit(solution)/shard_map/ppermute | solution.py:16
  50.0 28.2 %collective-permute-start.4 = (f32[32,64,128]{2,1,0:T(8,128)S(1)}, f32[32,64,128]{2,1,0:T(8,128)S(1)}, u32[]{:S(2)}, u32[]{:S(2)}) collective-permute-start(f32[32,64,128]{2,1,0:T(8,128)S(1)} %fusion.43), channel_id=1, source_target_pairs={{0,4},{4,8},{8,12},{12,16},{16,20},{20,24},{24,28},{28,0},{1,5},{5... | collective-permute-start | bytes 3145736 | tf_op jit(solution)/shard_map/while/body/eval_jaxpr/ppermute | solution.py:27
  51.8 11.1 %copy-start.1 = (f32[256,2048]{0,1:T(8,128)S(1)}, f32[256,2048]{0,1:T(8,128)}, u32[]{:S(2)}) copy-start(f32[256,2048]{0,1:T(8,128)} %copy.47) | copy-start | bytes 6291460
  62.9 15.3 %copy-start = (f32[512,2048]{0,1:T(8,128)S(1)}, f32[512,2048]{0,1:T(8,128)}, u32[]{:S(2)}) copy-start(f32[512,2048]{0,1:T(8,128)} %copy.53) | copy-start | bytes 12582916
